TPU v7x, 512 devices: a whole 4x8x8 slice. The times are simulated.
512 devices in a mesh: ctx: 64 (over z, x, core), head: 8 (over y).
Axes of the slice: x: 4, y: 8, z: 8, core: 2. Of those that a mesh axis runs over, the one named last changes fastest.
Arguments:
- queries: bfloat16 [8192, 36864], P('ctx', 'head'), may hold values from -6 to 6
- latents: bfloat16 [16384, 576], P('ctx'), may hold values from -5 to 5
- up_value: bfloat16 [512, 8192], P(None, 'head'), may hold values from -0.25 to 0.25
- grad_out: bfloat16 [8192, 8192], P('ctx', 'head'), may hold values from -12 to 12
- out_saved: bfloat16 [8192, 8192], P('ctx', 'head'), may hold values from -6 to 6
- log_sums: float32 [8192, 64], P('ctx', 'head'), as said below
- doc_starts: int32 [257], replicated, may hold values from 0 to 16384, as said below
Outputs:
- grad_queries: bfloat16 [8192, 36864], P('ctx', 'head')
- grad_latents: float32 [16384, 576], P(('ctx', 'head'))
- grad_up_value: float32 [512, 8192], P('ctx', 'head')
Inputs may be any that keep to these rules, and one draw needn't show every extreme that they name: doc_starts[0] is 0; the entries rise strictly until they reach 16384 and then stay at 16384; consecutive entries differ by at most 512, and some document has exactly 512 positions. log_sums[t, h] is the log of the sum of exp(score[t, h, s]) over the keys s allowed for query t, computed from these queries and latents.
All inputs are finite; a program needn't handle non-finite values.
Results may differ from a plain program's by a relative error of at most 0.0085.
Values may be sent and summed in bfloat16 or wider, within the bound.
A program may use at most 64 MiB of HBM per device.

v0:
```python
import jax
import jax.numpy as jnp
from jax import lax
from jax.sharding import PartitionSpec as P

SPAN = 2


softmax_scale = 192.0 ** (-0.5)


def passed_along(value, axis, steps):
    count = lax.axis_size(axis)
    first, last = (max(0, -steps), min(count, count - steps))
    return lax.ppermute(value, axis, [(source, source + steps) for source in range(first, last)])


def doc_index(positions, doc_starts):
    return jnp.sum((doc_starts[None, :] <= positions[:, None]).astype(jnp.int32), axis=1) - 1


def on_device(queries, latents, up_value, grad_out, out_saved, log_sums, doc_starts):
    query_rows = queries.shape[0]
    key_rows = latents.shape[0]
    feat_width = latents.shape[1]
    lat_width = up_value.shape[0]
    local_heads = log_sums.shape[1]
    value_width = grad_out.shape[1] // local_heads
    query_heads = queries.reshape(query_rows, local_heads, feat_width)
    grad_heads = grad_out.reshape(query_rows, local_heads, value_width)
    saved_heads = out_saved.reshape(query_rows, local_heads, value_width)
    weight_heads = up_value.reshape(lat_width, local_heads, value_width)
    device_pos = lax.axis_index("ctx")
    query_pos = (
        device_pos * key_rows + key_rows - query_rows + jnp.arange(query_rows, dtype=jnp.int32)
    )
    query_doc = doc_index(query_pos, doc_starts)
    grad_lat_q = jnp.einsum(
        "thv,jhv->thj", grad_heads, weight_heads, preferred_element_type=jnp.float32
    ).astype(jnp.bfloat16)
    row_delta = jnp.sum(grad_heads.astype(jnp.float32) * saved_heads.astype(jnp.float32), axis=2)

    def one_task(key_block, offset):
        key_pos = (device_pos - offset) * key_rows + jnp.arange(key_rows, dtype=jnp.int32)
        allowed = (query_doc[:, None] == doc_index(key_pos, doc_starts)[None, :]) & (
            key_pos[None, :] <= query_pos[:, None]
        )
        scores = (
            jnp.einsum("thf,sf->ths", query_heads, key_block, preferred_element_type=jnp.float32)
            * softmax_scale
        )
        prob_full = jnp.where(allowed[:, None, :], jnp.exp(scores - log_sums[:, :, None]), 0.0)
        prob_half = prob_full.astype(jnp.bfloat16)
        values = key_block[:, :lat_width]
        out_part = jnp.einsum("ths,sj->thj", prob_half, values, preferred_element_type=jnp.float32)
        grad_prob = jnp.einsum(
            "thj,sj->ths", grad_lat_q, values, preferred_element_type=jnp.float32
        )
        grad_score = (prob_full * (grad_prob - row_delta[:, :, None]) * softmax_scale).astype(
            jnp.bfloat16
        )
        query_part = jnp.einsum(
            "ths,sf->thf", grad_score, key_block, preferred_element_type=jnp.float32
        )
        grad_key = jnp.einsum(
            "ths,thf->sf", grad_score, query_heads, preferred_element_type=jnp.float32
        )
        grad_value = jnp.einsum(
            "ths,thj->sj", prob_half, grad_lat_q, preferred_element_type=jnp.float32
        )
        grad_key = grad_key + jnp.pad(grad_value, ((0, 0), (0, feat_width - lat_width)))
        return (out_part, query_part, grad_key)

    out_total, query_total, first_part = one_task(latents, 0)
    partials = [first_part]
    for offset in range(1, SPAN + 1):
        key_block = passed_along(latents, "ctx", offset)
        out_part, query_part, grad_key = one_task(key_block, offset)
        out_total = out_total + out_part
        query_total = query_total + query_part
        partials.append(grad_key)
    key_total = partials[0]
    for offset in range(1, SPAN + 1):
        key_total = key_total + passed_along(
            partials[offset].astype(jnp.bfloat16), "ctx", -offset
        ).astype(jnp.float32)
    grad_latents = lax.psum_scatter(key_total, "head", scatter_dimension=0, tiled=True)
    out_lat = out_total.astype(jnp.bfloat16)
    term_block = jnp.einsum("thj,thv->jhv", out_lat, grad_heads, preferred_element_type=jnp.float32)
    grad_up_value = lax.psum_scatter(
        term_block.reshape(
            lat_width // lax.axis_size("ctx") * lax.axis_size("ctx"), local_heads * value_width
        ),
        "ctx",
        scatter_dimension=0,
        tiled=True,
    )
    grad_queries = query_total.astype(jnp.bfloat16).reshape(query_rows, local_heads * feat_width)
    return (grad_queries, grad_latents, grad_up_value)


def solution(mesh):
    return jax.shard_map(
        on_device,
        mesh=mesh,
        in_specs=(
            P("ctx", "head"),
            P("ctx", None),
            P(None, "head"),
            P("ctx", "head"),
            P("ctx", "head"),
            P("ctx", "head"),
            P(),
        ),
        out_specs=(P("ctx", "head"), P(("ctx", "head"), None), P("ctx", "head")),
        check_vma=False,
    )
```

profile of v0, /device:TPU:1, one launch (start us, length us, event | category | flops | bytes accessed | tf_op | source)
XLA Modules:
  0.0 262.9 jit_solution(16536905302185326443)
XLA Ops:
  8.0 0.0 copy-start
  8.0 0.0 copy-start.14
  8.0 0.0 copy-start.13
  8.0 0.0 all-reduce.6.cloned.1.call-start
  8.1 4.6 %collective-permute-start = (bf16[256,576]{0,1:T(8,128)(2,1)}, bf16[256,576]{0,1:T(8,128)(2,1)}, u32[]{:S(2)}, u32[]{:S(2)}) collective-permute-start(bf16[256,576]{0,1:T(8,128)(2,1)} %param.8), channel_id=1, source_target_pairs={{0,8},{8,16},{16,24},{24,32},{32,40},{40,48},{48,56},{56,64},{64,7... | collective-permute-start | bytes 884744 | tf_op jit(solution)/shard_map/ppermute | solution.py:15
  12.7 3.9 %collective-permute-start.1 = (bf16[256,576]{0,1:T(8,128)(2,1)}, bf16[256,576]{0,1:T(8,128)(2,1)}, u32[]{:S(2)}, u32[]{:S(2)}) collective-permute-start(bf16[256,576]{0,1:T(8,128)(2,1)} %param.8), channel_id=1, source_target_pairs={{0,16},{8,24},{16,32},{24,40},{32,48},{40,56},{48,64},{56,72},{64,... | collective-permute-start | bytes 884744 | tf_op jit(solution)/shard_map/ppermute | solution.py:15
  16.6 0.0 copy-start.18
  16.6 0.8 convert_reduce_fusion
  17.5 0.0 copy-start.20
  17.5 0.8 convert_reduce_fusion.3
  18.3 0.6 broadcast_add_fusion.3
  18.8 1.7 copy.81
  20.6 0.2 copy.102
  20.9 0.0 copy-start.15
  20.9 0.1 copy.130
  21.0 0.2 multiply_reduce_fusion
  21.3 0.4 fusion
  21.8 0.2 copy-done.17
  22.0 0.0 copy-done.19
  22.0 0.8 compare_and_fusion
  22.8 0.0 copy-start.9
  22.8 1.7 fusion.4
  24.5 0.0 copy-start.2
  24.6 1.3 convolution_bitcast_fusion.5
  25.9 1.8 fusion.35
  27.7 0.0 collective-permute-done
  27.7 1.6 fusion.7
  29.3 0.5 convolution_bitcast_fusion.4
  29.8 1.5 fusion.18
  31.3 0.0 copy-start.4
  31.3 1.4 fusion.24
  32.7 4.4 %collective-permute-start.2 = (bf16[256,576]{1,0:T(8,128)(2,1)}, bf16[256,576]{1,0:T(8,128)(2,1)}, u32[]{:S(2)}, u32[]{:S(2)}) collective-permute-start(bf16[256,576]{1,0:T(8,128)(2,1)} %fusion.24), channel_id=1, source_target_pairs={{8,0},{16,8},{24,16},{32,24},{40,32},{48,40},{56,48},{64,56},{72,6... | collective-permute-start | bytes 884744 | tf_op jit(solution)/shard_map/ppermute | solution.py:15
  37.1 2.7 %fusion.41 = f32[128,8,512]{2,0,1:T(8,128)} fusion(f32[128,8,256]{2,0,1:T(8,128)S(1)} %fusion.7, bf16[256,576]{0,1:T(8,128)(2,1)} %collective-permute-done), kind=kOutput, calls=%fused_computation.63 | convolution fusion | flops 268697600 | bytes 3407872 | tf_op jit(solution)/shard_map/ths,sj->thj/dot_general | solution.py:55
  39.8 0.0 copy-done.4
  39.8 0.0 collective-permute-done.1
  39.8 2.6 %fusion.10 = f32[128,8,256]{2,0,1:T(8,128)} fusion(bf16[128,8,576]{0,2,1:T(8,128)(2,1)S(1)} %bitcast.100, f32[128,8]{0,1:T(8,128)S(1)} %copy-done.15, pred[128,256]{1,0:T(8,128)(4,1)S(1)} %get-tuple-element.18, bf16[256,576]{0,1:T(8,128)(2,1)} %collective-permute-done.1), kind=kOutput, calls=%fused_computation.16 | convolution fusion | flops 302776320 | bytes 2560000 | tf_op jit(solution)/shard_map/thf,sf->ths/dot_general | solution.py:49
  42.5 4.7 %fusion.1 = f32[8,512,128]{1,2,0:T(8,128)} fusion(bf16[128,8,128]{0,2,1:T(8,128)(2,1)S(1)} %copy.102, f32[128,8,512]{2,0,1:T(8,128)} %fusion.35, f32[128,8,512]{2,0,1:T(8,128)} %fusion.41, f32[128,8,256]{2,0,1:T(8,128)} %fusion.10, bf16[256,576]{0,1:T(8,128)(2,1)} %collective-permute-done.1), kind=kOutput, calls=%fused_computation.7 | convolution fusion | flops 404488192 | bytes 7864320 | tf_op jit(solution)/shard_map/thj,thv->jhv/dot_general | solution.py:89
  47.2 2.9 %copy.103 = f32[512,1024]{1,0:T(8,128)} copy(f32[512,1024]{0,1:T(8,128)} %bitcast.103) | data formatting | bytes 4194304 | tf_op jit(solution)/shard_map/reshape | solution.py:91
  50.1 0.0 all-reduce.6.cloned.1.call-update
  50.1 0.0 reduce-scatter.2.cloned.1.call-start
  50.2 1.9 fusion.19
  52.1 0.0 copy-start.3
  52.1 0.0 copy-start.10
  52.1 0.5 convolution_bitcast_fusion.3
  52.7 0.0 copy-start.12
  52.7 0.6 fusion.23
  53.3 1.5 collective-permute-start.3
  54.8 0.0 copy-done.3
  54.8 0.0 copy-done.10
  54.8 0.5 fusion.17
  55.3 0.0 copy-start.8
  55.3 0.0 copy-start.11
  55.3 0.0 collective-permute-done.2
  55.3 9.2 %collective-permute-done.3 = bf16[256,576]{1,0:T(8,128)(2,1)S(1)} collective-permute-done((bf16[256,576]{1,0:T(8,128)(2,1)S(1)}, bf16[256,576]{1,0:T(8,128)(2,1)S(1)}, u32[]{:S(2)}, u32[]{:S(2)}) %collective-permute-start.3) | collective-permute-done | bytes 294944 | tf_op jit(solution)/shard_map/ppermute | solution.py:15
  64.6 2.5 convert_add_fusion
  67.0 0.0 reduce-scatter.2.cloned.1.call-update
  67.1 1.3 dynamic-slice
  69.0 1.5 fusion.32
  70.6 1.5 fusion.29
  72.1 0.0 copy-done.7
  72.2 1.5 add_convert_fusion
  73.6 1.4 copy.104
  75.0 179.0 %all-reduce.6.cloned.1.call-done = f32[512,1024]{1,0:T(8,128)} async-done(((f32[512,1024]{1,0:T(8,128)}), f32[512,1024]{1,0:T(8,128)}) %all-reduce.6.cloned.1.call-update) | async-done | bytes 2097168
  254.1 1.4 constant_dynamic-slice_fusion
  (34 shorter events, 0.2 us)
Async XLA Ops:
  8.0 13.3 %copy-start = (bf16[512,1024]{1,0:T(8,128)(2,1)S(1)}, bf16[512,1024]{1,0:T(8,128)(2,1)}, u32[]{:S(2)}) copy-start(bf16[512,1024]{1,0:T(8,128)(2,1)} %param.9) | copy-start | bytes 3145732
  8.0 12.5 %copy-start.14 = (bf16[128,1024]{1,0:T(8,128)(2,1)S(1)}, bf16[128,1024]{1,0:T(8,128)(2,1)}, u32[]{:S(2)}) copy-start(bf16[128,1024]{1,0:T(8,128)(2,1)} %param.10) | copy-start | bytes 786436
  8.0 12.8 %copy-start.13 = (bf16[128,1024]{1,0:T(8,128)(2,1)S(1)}, bf16[128,1024]{1,0:T(8,128)(2,1)}, u32[]{:S(2)}) copy-start(bf16[128,1024]{1,0:T(8,128)(2,1)} %param.11) | copy-start | bytes 786436
  8.0 246.1 %all-reduce.6.cloned.1.call-start = ((), (), s32[]{:S(2)}) async-start(), calls=%async_computation.2 | async-start | bytes 4194304
  8.1 19.6 %collective-permute-start = (bf16[256,576]{0,1:T(8,128)(2,1)}, bf16[256,576]{0,1:T(8,128)(2,1)}, u32[]{:S(2)}, u32[]{:S(2)}) collective-permute-start(bf16[256,576]{0,1:T(8,128)(2,1)} %param.8), channel_id=1, source_target_pairs={{0,8},{8,16},{16,24},{24,32},{32,40},{40,48},{48,56},{56,64},{64,7... | collective-permute-start | bytes 884744 | tf_op jit(solution)/shard_map/ppermute | solution.py:15
  12.7 27.1 %collective-permute-start.1 = (bf16[256,576]{0,1:T(8,128)(2,1)}, bf16[256,576]{0,1:T(8,128)(2,1)}, u32[]{:S(2)}, u32[]{:S(2)}) collective-permute-start(bf16[256,576]{0,1:T(8,128)(2,1)} %param.8), channel_id=1, source_target_pairs={{0,16},{8,24},{16,32},{24,40},{32,48},{40,56},{48,64},{56,72},{64,... | collective-permute-start | bytes 884744 | tf_op jit(solution)/shard_map/ppermute | solution.py:15
  16.6 4.3 %copy-start.16 = (s32[256]{0:T(256)}, s32[256]{0:T(256)S(1)}, u32[]{:S(2)}) copy-start(s32[256]{0:T(256)S(1)} %iota_add_fusion) | copy-start | bytes 3076
  16.6 4.3 %copy-start.18 = (s32[256]{0:T(256)}, s32[256]{0:T(256)S(1)}, u32[]{:S(2)}) copy-start(s32[256]{0:T(256)S(1)} %iota_add_fusion.1) | copy-start | bytes 3076
  17.5 3.4 %copy-start.20 = (s32[128]{0:T(128)}, s32[128]{0:T(128)S(1)}, u32[]{:S(2)}) copy-start(s32[128]{0:T(128)S(1)} %iota_add_fusion.3) | copy-start | bytes 1540
  20.9 1.9 copy-start.15
  21.3 0.7 copy-start.17
  21.3 0.7 copy-start.19
  21.3 0.7 copy-start.21
  22.8 3.1 %copy-start.9 = (bf16[256,576]{0,1:T(8,128)(2,1)S(1)}, bf16[256,576]{0,1:T(8,128)(2,1)}, u32[]{:S(2)}) copy-start(bf16[256,576]{0,1:T(8,128)(2,1)} %param.8) | copy-start | bytes 884740
  24.5 3.1 %copy-start.2 = (f32[128,8,256]{2,0,1:T(8,128)}, f32[128,8,256]{2,0,1:T(8,128)S(1)}, u32[]{:S(2)}) copy-start(f32[128,8,256]{2,0,1:T(8,128)S(1)} %fusion.4) | copy-start | bytes 3145732
  31.3 8.5 %copy-start.4 = (bf16[128,8,256]{2,0,1:T(8,128)(2,1)}, bf16[128,8,256]{2,0,1:T(8,128)(2,1)S(1)}, u32[]{:S(2)}) copy-start(bf16[128,8,256]{2,0,1:T(8,128)(2,1)S(1)} %fusion.18) | copy-start | bytes 1572868
  32.7 22.6 %collective-permute-start.2 = (bf16[256,576]{1,0:T(8,128)(2,1)}, bf16[256,576]{1,0:T(8,128)(2,1)}, u32[]{:S(2)}, u32[]{:S(2)}) collective-permute-start(bf16[256,576]{1,0:T(8,128)(2,1)} %fusion.24), channel_id=1, source_target_pairs={{8,0},{16,8},{24,16},{32,24},{40,32},{48,40},{56,48},{64,56},{72,6... | collective-permute-start | bytes 884744 | tf_op jit(solution)/shard_map/ppermute | solution.py:15
  50.1 205.3 %reduce-scatter.2.cloned.1.call-start = ((), (), s32[]{:S(2)}) async-start(), calls=%async_computation.1 | async-start | bytes 737280 | tf_op jit(solution)/shard_map/reduce_scatter | solution.py:87
  50.2 1.9 copy-start.1
  52.1 1.2 copy-start.6
  52.1 2.7 %copy-start.3 = (f32[128,8,256]{2,0,1:T(8,128)S(1)}, f32[128,8,256]{2,0,1:T(8,128)}, u32[]{:S(2)}) copy-start(f32[128,8,256]{2,0,1:T(8,128)} %copy-done.2) | copy-start | bytes 3145732
  52.1 2.7 %copy-start.10 = (bf16[256,576]{0,1:T(8,128)(2,1)S(1)}, bf16[256,576]{0,1:T(8,128)(2,1)}, u32[]{:S(2)}) copy-start(bf16[256,576]{0,1:T(8,128)(2,1)} %param.8) | copy-start | bytes 884740
  52.7 11.9 %copy-start.12 = (f32[256,512]{1,0:T(8,128)S(1)}, f32[256,512]{1,0:T(8,128)}, u32[]{:S(2)}) copy-start(f32[256,512]{1,0:T(8,128)} %convolution_bitcast_fusion.5) | copy-start | bytes 1572868
  53.3 11.3 %collective-permute-start.3 = (bf16[256,576]{1,0:T(8,128)(2,1)S(1)}, bf16[256,576]{1,0:T(8,128)(2,1)S(1)}, u32[]{:S(2)}, u32[]{:S(2)}) collective-permute-start(bf16[256,576]{1,0:T(8,128)(2,1)S(1)} %fusion.23), channel_id=1, source_target_pairs={{16,0},{24,8},{32,16},{40,24},{48,32},{56,40},{64,48},{72,56},{80,... | collective-permute-start | bytes 884744 | tf_op jit(solution)/shard_map/ppermute | solution.py:15
  55.3 9.3 %copy-start.8 = (bf16[128,8,256]{2,0,1:T(8,128)(2,1)}, bf16[128,8,256]{2,0,1:T(8,128)(2,1)S(1)}, u32[]{:S(2)}) copy-start(bf16[128,8,256]{2,0,1:T(8,128)(2,1)S(1)} %fusion.17) | copy-start | bytes 1572868
  55.3 13.7 %copy-start.11 = (bf16[256,576]{0,1:T(8,128)(2,1)S(1)}, bf16[256,576]{0,1:T(8,128)(2,1)}, u32[]{:S(2)}) copy-start(bf16[256,576]{0,1:T(8,128)(2,1)} %param.8) | copy-start | bytes 884740
  67.0 3.6 %copy-start.5 = (bf16[128,8,256]{2,0,1:T(8,128)(2,1)S(1)}, bf16[128,8,256]{2,0,1:T(8,128)(2,1)}, u32[]{:S(2)}) copy-start(bf16[128,8,256]{2,0,1:T(8,128)(2,1)} %copy-done.4) | copy-start | bytes 1572868
  70.6 1.5 copy-start.7
Sparse Core Ops, SparseCore 0:
  50.3 203.7 all-reduce.5
Sparse Core Ops, SparseCore 1:
  67.1 39.8 reduce-scatter.1
where the time goes:
time: 264 us; the launch traced here: 263 us
  waiting for transfers between devices  188 us (71%)
  matrix products  30.9 us (12%)
  between operations  16.6 us (6%)
  starting transfers between devices  14.4 us (5%)
  local copies, waits for them, and re-layouts  9.47 us (4%)
  other arithmetic  3.26 us (1%)
    unnamed x3, waiting for transfers between devices  179 us
    ppermute x4, starting transfers between devices, passed_along(): lax.ppermute(value, axis, [(source, source + steps) for source in range(f...  14.3 us
    ppermute x4, waiting for transfers between devices, passed_along(): lax.ppermute(value, axis, [(source, source + steps) for source in range(f...  9.23 us
    unnamed x50, local copies, waits for them, and re-layouts  6.29 us
    dot_general x3, matrix products, one_task(): jnp.einsum('thf,sf->ths', query_heads, key_block, preferred_element_type=...  5.99 us
  transfers between devices with their start and end apart: 6, of which 2 were waited for; matrix products, arithmetic and copies ran while one was open for 16% of the time, Pallas kernels for 0%

commit v1 on v0

v1 whole, which is shorter than its diff:
```python
import functools

import jax
import jax.numpy as jnp
from jax import lax
from jax.experimental import pallas as pl
from jax.experimental.pallas import tpu as pltpu
from jax.sharding import PartitionSpec as P

SCALE = 192.0 ** (-0.5)
MESH = pl.DeviceIdType.MESH
NX, NZ, NC, NY = 4, 8, 2, 8
CTX = NX * NZ * NC
F32, BF16 = jnp.float32, jnp.bfloat16


def dot(a, b, ca, cb):
    return lax.dot_general(a, b, (((ca,), (cb,)), ((), ())), preferred_element_type=F32)


def barrier(peers):
    sem = pltpu.get_barrier_semaphore()
    for peer in peers:
        pl.semaphore_signal(sem, inc=1, device_id=peer, device_id_type=MESH)
    pl.semaphore_wait(sem, len(peers))


def shift_kernel(own_ref, prev_ref, send_sem, recv_sem):
    d, y = lax.axis_index("ctx"), lax.axis_index("head")
    at = lambda step: (lax.rem(d + step + CTX, CTX), y)
    barrier([at(1), at(-1), at(2), at(-2)])
    near = pltpu.make_async_remote_copy(
        own_ref, prev_ref.at[pl.ds(128, 256)], send_sem.at[0], recv_sem.at[0], at(1), MESH
    )
    far = pltpu.make_async_remote_copy(
        own_ref.at[pl.ds(128, 128)], prev_ref.at[pl.ds(0, 128)], send_sem.at[1], recv_sem.at[1],
        at(2), MESH,
    )
    near.start()
    far.start()
    near.wait()
    far.wait()


def shift(latents):
    return pl.pallas_call(
        shift_kernel,
        out_shape=jax.ShapeDtypeStruct((384, 576), BF16),
        in_specs=[pl.BlockSpec(memory_space=pltpu.VMEM)],
        out_specs=pl.BlockSpec(memory_space=pltpu.VMEM),
        scratch_shapes=[pltpu.SemaphoreType.DMA((2,)), pltpu.SemaphoreType.DMA((2,))],
        compiler_params=pltpu.CompilerParams(collective_id=0, has_side_effects=True),
        name="shift",
    )(latents)


def compute_kernel(
    q_ref, own_ref, prev_ref, w_ref, g_ref, o_ref, ls_ref, ds_ref,
    gq_ref, gkp_ref, gko_ref, t_ref,
    ck, qs, gl, pb, gs, gqs, ol, gk,
):
    d = lax.axis_index("ctx")
    ck[0, pl.ds(0, 384), pl.ds(0, 576)] = prev_ref[...]
    ck[0, pl.ds(384, 256), pl.ds(0, 576)] = own_ref[...]
    ck[0, :, pl.ds(576, 64)] = jnp.zeros((640, 64), BF16)
    ck[1] = pltpu.roll(ck[0].astype(F32), 64, 1).astype(BF16)

    qpos = d * 256 + 128 + lax.broadcasted_iota(jnp.int32, (128, 1), 0)
    starts = ds_ref[...]
    begin = jnp.max(jnp.where(starts <= qpos, starts, 0), axis=1, keepdims=True)
    kpos = d * 256 - 384 + lax.broadcasted_iota(jnp.int32, (128, 640), 1)
    allowed = (kpos >= begin) & (kpos <= qpos)

    for par in range(2):
        for i in range(4):
            rows = pl.ds(i * 128, 128)
            h = 2 * i + par
            qs[par, rows, :] = q_ref[:, pl.ds(i * 1152 + par * 512, 640)]
            gl[par, rows, :] = dot(
                g_ref[:, pl.ds(h * 128, 128)], w_ref[:, pl.ds(h * 128, 128)], 1, 1
            ).astype(BF16)

    for par in range(2):
        score = dot(qs[par], ck[par], 1, 1)
        gprob = dot(gl[par], ck[0, :, pl.ds(0, 512)], 1, 1)
        for i in range(4):
            rows = pl.ds(i * 128, 128)
            h = 2 * i + par
            cols = pl.ds(h * 128, 128)
            delta = jnp.sum(
                g_ref[:, cols].astype(F32) * o_ref[:, cols].astype(F32), axis=1, keepdims=True
            )
            part = slice(i * 128, (i + 1) * 128)
            prob = jnp.where(allowed, jnp.exp(score[part] * SCALE - ls_ref[:, pl.ds(h, 1)]), 0.0)
            pb[par, rows, :] = prob.astype(BF16)
            gs[par, rows, :] = (prob * (gprob[part] - delta) * SCALE).astype(BF16)
        ol[par] = dot(pb[par], ck[0, :, pl.ds(0, 512)], 1, 0).astype(BF16)
        gqs[par] = dot(gs[par], ck[par], 1, 0)
        gk[par] = dot(gs[par], qs[par], 0, 0)
        gk[0, :, pl.ds(0, 512)] += dot(pb[par], gl[par], 0, 0)
        for i in range(4):
            h = 2 * i + par
            term = dot(
                ol[par, pl.ds(i * 128, 128), :], g_ref[:, pl.ds(h * 128, 128)], 0, 0
            ).astype(BF16)
            term = term.reshape(NZ, NX, 16, 128)
            for x in range(NX):
                t_ref[h // 4, x, :, :, pl.ds((h % 4) * 128, 128)] = term[:, x]

    for i in range(4):
        rows = pl.ds(i * 128, 128)
        even, odd = gqs[0, rows, :], gqs[1, rows, :]
        gq_ref[:, pl.ds(i * 1152, 512)] = even[:, :512].astype(BF16)
        gq_ref[:, pl.ds(i * 1152 + 512, 128)] = (even[:, 512:] + odd[:, :128]).astype(BF16)
        gq_ref[:, pl.ds(i * 1152 + 640, 512)] = odd[:, 128:].astype(BF16)
    total = gk[0] + pltpu.roll(gk[1], 576, 1)
    gkp_ref[...] = total[:384, :576].astype(BF16)
    gko_ref[...] = total[384:, :576]


def compute(queries, own, prev, up_value, grad_out, out_saved, log_sums, doc_starts):
    vmem = pl.BlockSpec(memory_space=pltpu.VMEM)
    return pl.pallas_call(
        compute_kernel,
        out_shape=(
            jax.ShapeDtypeStruct((128, 4608), BF16),
            jax.ShapeDtypeStruct((384, 576), BF16),
            jax.ShapeDtypeStruct((256, 576), F32),
            jax.ShapeDtypeStruct((2, NX, NZ, 16, 512), BF16),
        ),
        in_specs=[vmem] * 8,
        out_specs=(vmem,) * 4,
        scratch_shapes=[
            pltpu.VMEM((2, 640, 640), BF16),
            pltpu.VMEM((2, 512, 640), BF16),
            pltpu.VMEM((2, 512, 512), BF16),
            pltpu.VMEM((2, 512, 640), BF16),
            pltpu.VMEM((2, 512, 640), BF16),
            pltpu.VMEM((2, 512, 640), F32),
            pltpu.VMEM((2, 512, 512), BF16),
            pltpu.VMEM((2, 640, 640), F32),
        ],
        compiler_params=pltpu.CompilerParams(vmem_limit_bytes=56 << 20),
        name="attend",
    )(queries, own, prev, up_value, grad_out, out_saved, log_sums, doc_starts)


def reduce_kernel(
    gkp_ref, gko_ref, t_ref, gl_ref, gw_ref,
    back_near, back_far, ysend, yrecv, crecv, xsend, xrecv, zsend, zrecv, fin, frecv,
    s_back, r_back, s_y, r_y, s_c, r_c, s_x, r_x, s_z, r_z, s_f, r_f,
):
    d, y = lax.axis_index("ctx"), lax.axis_index("head")
    z, x, c = d // 8, lax.rem(d // 2, 4), lax.rem(d, 2)
    ring = lambda step: (lax.rem(d + step + CTX, CTX), y)
    partner = (d + 1 - 2 * c, y)
    at_x = lambda step: (z * 8 + lax.rem(x + step, 4) * 2 + c, y)
    at_z = lambda step: (lax.rem(z + step, 8) * 8 + x * 2 + c, y)
    at_y = lambda step: (d, lax.rem(y + step, 8))
    barrier(
        [ring(1), ring(-1), ring(2), ring(-2), partner]
        + [at_x(k) for k in range(1, NX)]
        + [at_z(k) for k in range(1, NZ)]
        + [at_y(k) for k in range(1, NY)]
    )

    def remote(src, dst, send, recv, to):
        copy = pltpu.make_async_remote_copy(src, dst, send, recv, to, MESH)
        copy.start()
        return copy

    near = remote(gkp_ref.at[pl.ds(128, 256)], back_near, s_back.at[0], r_back.at[0], ring(-1))
    far = remote(gkp_ref.at[pl.ds(0, 128)], back_far, s_back.at[1], r_back.at[1], ring(-2))
    cores = []
    for k in range(1, NX + 1):
        xi = lax.rem(x + k, 4)
        cores.append(
            remote(t_ref.at[1 - c, xi], crecv.at[xi], s_c.at[k - 1], r_c.at[k - 1], partner)
        )

    xs = []
    for k in range(1, NX):
        xi = lax.rem(x + k, 4)
        cores[k - 1].wait_recv()
        xsend[k - 1] = (t_ref[c, xi].astype(F32) + crecv[xi].astype(F32)).astype(BF16)
        xs.append(remote(xsend.at[k - 1], xrecv.at[k - 1], s_x.at[k - 1], r_x.at[k - 1], at_x(k)))

    near.wait_recv()
    far.wait_recv()
    total = gko_ref[...] + back_near[...].astype(F32)
    total = jnp.concatenate([total[:128], total[128:] + back_far[...].astype(F32)], axis=0)
    ysend[...] = total.astype(BF16).reshape(NY, 32, 576)
    ys = []
    for k in range(1, NY):
        ys.append(
            remote(
                ysend.at[lax.rem(y + k, 8)], yrecv.at[k - 1], s_y.at[k - 1], r_y.at[k - 1], at_y(k)
            )
        )

    cores[NX - 1].wait_recv()
    part = t_ref[c, x].astype(F32) + crecv[x].astype(F32)
    for k in range(1, NX):
        xs[k - 1].wait_recv()
        part = part + xrecv[k - 1].astype(F32)
    zsend[...] = part.astype(BF16)
    zs = []
    for k in range(1, NZ):
        zs.append(
            remote(
                zsend.at[lax.rem(z + k, 8)], zrecv.at[k - 1], s_z.at[k - 1], r_z.at[k - 1], at_z(k)
            )
        )

    mine = ysend[y].astype(F32)
    for k in range(1, NY):
        ys[k - 1].wait_recv()
        mine = mine + yrecv[k - 1].astype(F32)
    gl_ref[...] = mine

    last = zsend[z].astype(F32)
    for k in range(1, NZ):
        zs[k - 1].wait_recv()
        last = last + zrecv[k - 1].astype(F32)
    fin[...] = last.reshape(2, 8, 512)
    swap = remote(fin.at[1 - c], frecv, s_f, r_f, partner)
    gw_ref[:, pl.ds(pl.multiple_of(c * 512, 512), 512)] = fin[c]
    swap.wait_recv()
    gw_ref[:, pl.ds(pl.multiple_of((1 - c) * 512, 512), 512)] = frecv[...]
    for copy in [near, far, swap] + cores + xs + ys + zs:
        copy.wait_send()


def reduce(gk_prev, gk_own, terms):
    vmem = pl.BlockSpec(memory_space=pltpu.VMEM)
    dma = pltpu.SemaphoreType.DMA
    return pl.pallas_call(
        reduce_kernel,
        out_shape=(
            jax.ShapeDtypeStruct((32, 576), F32),
            jax.ShapeDtypeStruct((8, 1024), F32),
        ),
        in_specs=[vmem] * 3,
        out_specs=(vmem,) * 2,
        scratch_shapes=[
            pltpu.VMEM((256, 576), BF16),
            pltpu.VMEM((128, 576), BF16),
            pltpu.VMEM((NY, 32, 576), BF16),
            pltpu.VMEM((NY - 1, 32, 576), BF16),
            pltpu.VMEM((NX, NZ, 16, 512), BF16),
            pltpu.VMEM((NX - 1, NZ, 16, 512), BF16),
            pltpu.VMEM((NX - 1, NZ, 16, 512), BF16),
            pltpu.VMEM((NZ, 16, 512), BF16),
            pltpu.VMEM((NZ - 1, 16, 512), BF16),
            pltpu.VMEM((2, 8, 512), F32),
            pltpu.VMEM((8, 512), F32),
            dma((2,)), dma((2,)),
            dma((NY - 1,)), dma((NY - 1,)),
            dma((NX,)), dma((NX,)),
            dma((NX - 1,)), dma((NX - 1,)),
            dma((NZ - 1,)), dma((NZ - 1,)),
            dma, dma,
        ],
        compiler_params=pltpu.CompilerParams(
            collective_id=1, has_side_effects=True, vmem_limit_bytes=32 << 20
        ),
        name="reduce",
    )(gk_prev, gk_own, terms)


def on_device(queries, latents, up_value, grad_out, out_saved, log_sums, doc_starts):
    prev = shift(latents)
    grad_queries, gk_prev, gk_own, terms = compute(
        queries, latents, prev, up_value, grad_out, out_saved, log_sums, doc_starts.reshape(1, -1)
    )
    grad_latents, grad_up_value = reduce(gk_prev, gk_own, terms)
    return (grad_queries, grad_latents, grad_up_value)


def solution(mesh):
    return jax.shard_map(
        on_device,
        mesh=mesh,
        in_specs=(
            P("ctx", "head"),
            P("ctx", None),
            P(None, "head"),
            P("ctx", "head"),
            P("ctx", "head"),
            P("ctx", "head"),
            P(),
        ),
        out_specs=(P("ctx", "head"), P(("ctx", "head"), None), P("ctx", "head")),
        check_vma=False,
    )
```

time: 264 us -> 69.7 us (0.26)
  waiting for transfers between devices: 188 us -> 0 us
  Pallas kernels: 0 us -> 58.8 us
  matrix products: 30.9 us -> 0 us
  between operations: 16.6 us -> 0.65 us
  starting transfers between devices: 14.4 us -> 0 us
  other arithmetic: 3.26 us -> 0 us
    unnamed x3 -> x0, waiting for transfers between devices: 179 us -> none
    pallas_call x0 -> x3, Pallas kernels: none -> 58.8 us  [the longest x1 25.9 us: reduce(): pl.pallas_call(reduce_kernel, out_shape=(jax.ShapeDtypeStruct((32, 576),...]
    dot_general x19 -> x0, matrix products: 30.9 us -> none  [the longest x3 5.99 us: one_task(): jnp.einsum('thf,sf->ths', query_heads, key_block, preferred_element_type=...]
    ppermute x4 -> x0, starting transfers between devices: 14.3 us -> none  [passed_along(): lax.ppermute(value, axis, [(source, source + steps) for source in range(f...]
    ppermute x4 -> x0, waiting for transfers between devices: 9.23 us -> none  [passed_along(): lax.ppermute(value, axis, [(source, source + steps) for source in range(f...]
    unnamed x50 -> x10, local copies, waits for them, and re-layouts: 6.29 us -> 7.88 us
  transfers between devices with their start and end apart: 6 -> 0, of which waited for: 2 -> 0; matrix products, arithmetic and copies ran while one was open for 16% -> 0% of each run, Pallas kernels for 0% -> 0%
where the time goes in v1:
time: 69.7 us; the launch traced here: 68.5 us
  Pallas kernels  58.8 us (84%)
  local copies, waits for them, and re-layouts  9.13 us (13%)
    pallas_call x1, Pallas kernels, reduce(): pl.pallas_call(reduce_kernel, out_shape=(jax.ShapeDtypeStruct((32, 576),...  25.9 us
    pallas_call x1, Pallas kernels, shift(): pl.pallas_call(shift_kernel, out_shape=jax.ShapeDtypeStruct((384, 576), B...  22.9 us
    pallas_call x1, Pallas kernels, compute(): pl.pallas_call(compute_kernel, out_shape=(jax.ShapeDtypeStruct((128, 4608...  9.92 us
    unnamed x10, local copies, waits for them, and re-layouts  7.88 us

profile of v1, /device:TPU:1, one launch (start us, length us, event | category | flops | bytes accessed | tf_op | source)
XLA Modules:
  0.0 68.5 jit_solution(17511441625506890515)
XLA Ops:
  0.6 1.2 %reshape.9.ds_ref = s32[1,257]{1,0:T(1,128)} reshape(s32[257]{0:T(512)} %param.13) | data formatting | bytes 2056 | tf_op jit(solution)/shard_map/reshape | solution.py:274
  1.9 1.4 %copy.12.ls_ref = f32[128,8]{1,0:T(8,128)} copy(f32[128,8]{0,1:T(8,128)} %param.12) | data formatting | bytes 8192 | tf_op args[5]
  3.3 1.9 %copy.11.own_ref = bf16[256,576]{1,0:T(8,128)(2,1)} copy(bf16[256,576]{0,1:T(8,128)(2,1)} %param.8) | data formatting | bytes 589824 | tf_op args[1]
  5.2 22.9 %shift.1.prev_ref = bf16[384,576]{1,0:T(8,128)(2,1)} custom-call(bf16[256,576]{1,0:T(8,128)(2,1)} %copy.11.own_ref), custom_call_target="tpu_custom_call" | custom-call | tf_op jit(solution)/shard_map/shift/pallas_call | solution.py:46
  28.1 9.9 %attend.1 = (bf16[128,4608]{1,0:T(8,128)(2,1)}, bf16[384,576]{1,0:T(8,128)(2,1)}, f32[256,576]{1,0:T(8,128)}, bf16[2,4,8,16,512]{4,3,2,1,0:T(8,128)(2,1)}) custom-call(bf16[128,4608]{1,0:T(8,128)(2,1)} %q_ref.1, bf16[256,576]{1,0:T(8,128)(2,1)} %copy.11.own_ref, bf16[384,576]{1,0:T(8,128)(2,1)} %shift.1.prev_ref, bf16[512,1024]{1,0:T(8,128)(2,1)} %w_ref.1, ...), custom_call_target="tpu_custom_call" | custom-call | tf_op jit(solution)/shard_map/attend/pallas_call | solution.py:123
  38.0 0.0 copy-start
  38.0 1.2 %copy-done = bf16[2,4,8,16,512]{4,3,2,1,0:T(8,128)(2,1)S(1)} copy-done((bf16[2,4,8,16,512]{4,3,2,1,0:T(8,128)(2,1)S(1)}, bf16[2,4,8,16,512]{4,3,2,1,0:T(8,128)(2,1)}, u32[]{:S(2)}) %copy-start) | copy-done | bytes 1048600
  39.2 0.0 copy-start.1
  39.2 1.1 %copy-done.1 = f32[256,576]{1,0:T(8,128)S(1)} copy-done((f32[256,576]{1,0:T(8,128)S(1)}, f32[256,576]{1,0:T(8,128)}, u32[]{:S(2)}) %copy-start.1) | copy-done | bytes 589848
  40.3 0.0 copy-start.2
  40.3 1.0 %copy-done.2 = bf16[384,576]{1,0:T(8,128)(2,1)S(1)} copy-done((bf16[384,576]{1,0:T(8,128)(2,1)S(1)}, bf16[384,576]{1,0:T(8,128)(2,1)}, u32[]{:S(2)}) %copy-start.2) | copy-done | bytes 442392
  41.3 25.9 %reduce.1 = (f32[32,576]{1,0:T(8,128)S(1)}, f32[8,1024]{1,0:T(8,128)S(1)}) custom-call(bf16[384,576]{1,0:T(8,128)(2,1)S(1)} %copy-done.2, f32[256,576]{1,0:T(8,128)S(1)} %copy-done.1, bf16[2,4,8,16,512]{4,3,2,1,0:T(8,128)(2,1)S(1)} %copy-done), custom_call_target="tpu_custom_call" | custom-call | tf_op jit(solution)/shard_map/reduce/pallas_call | solution.py:237
  67.3 0.6 copy.15
  67.9 0.6 copy.16
Async XLA Ops:
  38.0 1.2 %copy-start = (bf16[2,4,8,16,512]{4,3,2,1,0:T(8,128)(2,1)S(1)}, bf16[2,4,8,16,512]{4,3,2,1,0:T(8,128)(2,1)}, u32[]{:S(2)}) copy-start(bf16[2,4,8,16,512]{4,3,2,1,0:T(8,128)(2,1)} %get-tuple-element.12.t_ref) | copy-start | bytes 3145732
  39.2 1.1 %copy-start.1 = (f32[256,576]{1,0:T(8,128)S(1)}, f32[256,576]{1,0:T(8,128)}, u32[]{:S(2)}) copy-start(f32[256,576]{1,0:T(8,128)} %get-tuple-element.11.gko_ref) | copy-start | bytes 1769476
  40.3 1.0 %copy-start.2 = (bf16[384,576]{1,0:T(8,128)(2,1)S(1)}, bf16[384,576]{1,0:T(8,128)(2,1)}, u32[]{:S(2)}) copy-start(bf16[384,576]{1,0:T(8,128)(2,1)} %get-tuple-element.10.gkp_ref) | copy-start | bytes 1327108

commit v2 on v0

v2 whole, which is shorter than its diff:
```python
import jax
import jax.numpy as jnp
from jax import lax
from jax.experimental import pallas as pl
from jax.experimental.pallas import tpu as pltpu
from jax.sharding import PartitionSpec as P

SCALE = 192.0 ** (-0.5)
MESH = pl.DeviceIdType.MESH
NX, NZ, NC, NY = 4, 8, 2, 8
CTX = NX * NZ * NC
F32, BF16 = jnp.float32, jnp.bfloat16
OWN, NEAR, FAR = (0, 256), (256, 256), (512, 128)


def dot(a, b, ca, cb):
    return lax.dot_general(a, b, (((ca,), (cb,)), ((), ())), preferred_element_type=F32)


def kernel(
    q_hbm, ct_hbm, w_hbm, g_hbm, o_hbm, ls_hbm, ds_ref,
    gq_hbm, gl_ref, gw_ref,
    qv, wv, gv, ov, lsv, win, qs, gl, pb, gs, ol, gqv, delta, lsc,
    gko, nbuf, nrecv, ya, yarecv, yb, ybrecv, ybsum, bsend, brecv,
    tv, crecv, xsend, xrecv, zpart, zsend, zrecv, fin, frecv,
    s_in, s_out, s_sh, r_sh, s_n, r_n, s_ya, r_ya, s_yb, r_yb, s_b, r_b,
    s_c, r_c, s_x, r_x, s_z, r_z, s_f, r_f,
):
    d, y = lax.axis_index("ctx"), lax.axis_index("head")
    z, x, c = d // 8, lax.rem(d // 2, 4), lax.rem(d, 2)
    ring = lambda step: (lax.rem(d + step + CTX, CTX), y)
    partner = (d + 1 - 2 * c, y)
    at_x = lambda step: (z * 8 + lax.rem(x + step, 4) * 2 + c, y)
    at_z = lambda step: (lax.rem(z + step, 8) * 8 + x * 2 + c, y)
    at_y = lambda step: (d, lax.rem(y + step, 8))

    def remote(src, dst, send, recv, to):
        return pltpu.make_async_remote_copy(src, dst, send, recv, to, MESH)

    feats = pl.ds(64, 576)
    loads = [
        pltpu.make_async_copy(ct_hbm, win.at[feats, pl.ds(0, 256)], s_in.at[0]),
        pltpu.make_async_copy(g_hbm, gv, s_in.at[1]),
        pltpu.make_async_copy(w_hbm, wv, s_in.at[2]),
        pltpu.make_async_copy(q_hbm, qv, s_in.at[3]),
        pltpu.make_async_copy(ls_hbm, lsv, s_in.at[4]),
        pltpu.make_async_copy(o_hbm, ov, s_in.at[5]),
    ]
    for load in loads:
        load.start()

    peers = (
        [ring(1), ring(-1), ring(2), ring(-2), partner]
        + [at_x(k) for k in range(1, NX)]
        + [at_y(k) for k in range(1, NY)]
        + [at_z(k) for k in range(1, NZ)]
    )
    entry = pltpu.get_barrier_semaphore()
    for peer in peers:
        pl.semaphore_signal(entry, inc=1, device_id=peer, device_id_type=MESH)
    win[pl.ds(0, 64), :] = jnp.zeros((64, 640), BF16)
    win[pl.ds(640, 64), :] = jnp.zeros((64, 640), BF16)
    loads[0].wait()
    pl.semaphore_wait(entry, len(peers))
    near = remote(
        win.at[feats, pl.ds(0, 256)], win.at[feats, pl.ds(256, 256)], s_sh.at[0], r_sh.at[0],
        ring(1),
    )
    far = remote(
        win.at[feats, pl.ds(128, 128)], win.at[feats, pl.ds(512, 128)], s_sh.at[1], r_sh.at[1],
        ring(2),
    )
    near.start()
    far.start()

    for load in loads[1:]:
        load.wait()
    lsc[...] = lsv[...].T
    for par in range(2):
        for i in range(4):
            rows = pl.ds(i * 128, 128)
            h = 2 * i + par
            cols = pl.ds(h * 128, 128)
            qs[par, rows, :] = qv[:, pl.ds(i * 1152 + par * 512, 640)]
            gl[par, rows, :] = dot(gv[:, cols], wv[:, cols], 1, 1).astype(BF16)
            delta[:, pl.ds(h, 1)] = jnp.sum(
                gv[:, cols].astype(F32) * ov[:, cols].astype(F32), axis=1, keepdims=True
            )
    qpos = d * 256 + 128 + lax.broadcasted_iota(jnp.int32, (128, 1), 0)
    starts = ds_ref[...]
    begin = jnp.max(jnp.where(starts <= qpos, starts, 0), axis=1, keepdims=True)

    def attend(par, block, base):
        first, count = block
        lanes = pl.ds(first, count)
        score = dot(qs[par], win[pl.ds(64 - 64 * par, 640), lanes], 1, 0)
        gprob = dot(gl[par], win[pl.ds(64, 512), lanes], 1, 0)
        kpos = base + lax.broadcasted_iota(jnp.int32, (128, count), 1)
        allowed = (kpos >= begin) & (kpos <= qpos)
        for i in range(4):
            rows = pl.ds(i * 128, 128)
            part = slice(i * 128, (i + 1) * 128)
            h = pl.ds(2 * i + par, 1)
            prob = jnp.where(allowed, jnp.exp(score[part] * SCALE - lsc[:, h]), 0.0)
            pb[par, rows, lanes] = prob.astype(BF16)
            gs[par, rows, lanes] = (prob * (gprob[part] - delta[:, h]) * SCALE).astype(BF16)
        part = dot(pb[par, :, lanes], win[pl.ds(64, 512), lanes], 1, 1)
        return part

    def key_grad(block):
        lanes = pl.ds(*block)
        even = dot(gs[0, :, lanes], qs[0], 0, 0)
        odd = pltpu.roll(dot(gs[1, :, lanes], qs[1], 0, 0), 576, 1)
        value = dot(pb[0, :, lanes], gl[0], 0, 0) + dot(pb[1, :, lanes], gl[1], 0, 0)
        both = even + odd
        return jnp.concatenate([both[:, :512] + value, both[:, 512:576]], axis=1)

    for par in range(2):
        ol[par] = attend(par, OWN, d * 256)
    gko[...] = key_grad(OWN)

    near.wait_recv()
    for par in range(2):
        ol[par] += attend(par, NEAR, d * 256 - 256)
    far.wait_recv()

    cores, xs, zs, swaps = [[], []], [[], []], [[], []], []

    def up_grad(par):
        lat = (ol[par] + attend(par, FAR, d * 256 - 384)).astype(BF16)
        for i in range(4):
            h = 2 * i + par
            term = dot(lat[i * 128 : (i + 1) * 128], gv[:, pl.ds(h * 128, 128)], 0, 0)
            term = term.astype(BF16).reshape(NZ, NX, 16, 128)
            for xi in range(NX):
                tv[par, i // 2, xi, :, :, pl.ds((i % 2) * 128, 128)] = term[:, xi]
        for k in range(1, NX + 1):
            xi = lax.rem(x + k, 4)
            j = par * NX + k - 1
            copy = remote(
                tv.at[par, 1 - c, xi], crecv.at[par, xi], s_c.at[j], r_c.at[j], partner
            )
            copy.start()
            cores[par].append(copy)

    def stage_x(par):
        for k in range(1, NX):
            xi = lax.rem(x + k, 4)
            j = par * (NX - 1) + k - 1
            cores[par][k - 1].wait_recv()
            xsend[j] = (tv[par, c, xi].astype(F32) + crecv[par, xi].astype(F32)).astype(BF16)
            copy = remote(xsend.at[j], xrecv.at[j], s_x.at[j], r_x.at[j], at_x(k))
            copy.start()
            xs[par].append(copy)
        cores[par][NX - 1].wait_recv()
        zpart[par] = tv[par, c, x].astype(F32) + crecv[par, x].astype(F32)

    def stage_z(par):
        part = zpart[par]
        for k in range(1, NX):
            xs[par][k - 1].wait_recv()
            part = part + xrecv[par * (NX - 1) + k - 1].astype(F32)
        zsend[par] = part.astype(BF16)
        for k in range(1, NZ):
            j = par * (NZ - 1) + k - 1
            copy = remote(
                zsend.at[par, lax.rem(z + k, 8)], zrecv.at[j], s_z.at[j], r_z.at[j], at_z(k)
            )
            copy.start()
            zs[par].append(copy)

    def stage_swap(par):
        last = zsend[par, z].astype(F32)
        for k in range(1, NZ):
            zs[par][k - 1].wait_recv()
            last = last + zrecv[par * (NZ - 1) + k - 1].astype(F32)
        fin[par] = last.reshape(2, 8, 256)
        copy = remote(fin.at[par, 1 - c], frecv.at[par], s_f.at[par], r_f.at[par], partner)
        copy.start()
        swaps.append(copy)

    up_grad(0)
    up_grad(1)
    stage_x(0)

    near_grad = key_grad(NEAR)
    nbuf[...] = near_grad.astype(BF16)
    whole = remote(nbuf, nrecv, s_n, r_n, partner)
    half = remote(
        nbuf.at[pl.ds(128, 128)], nrecv.at[pl.ds(0, 128)], s_n, r_n, partner
    )

    @pl.when(c == 1)
    def _():
        whole.start()

    @pl.when(c == 0)
    def _():
        half.start()

    stage_x(1)
    gkf = key_grad(FAR)
    yb[pl.ds(0, 4)] = near_grad[:128].reshape(4, 32, 576).astype(BF16)

    @pl.when(c == 0)
    def _():
        whole.wait_recv()
        gko[...] += nrecv[...].astype(F32)
        yb[pl.ds(4, 4)] = gkf.reshape(4, 32, 576).astype(BF16)

    @pl.when(c == 1)
    def _():
        half.wait_recv()
        yb[pl.ds(4, 4)] = (
            (gkf + nrecv[pl.ds(0, 128)].astype(F32)).reshape(4, 32, 576).astype(BF16)
        )

    ybs, yas = [], []
    for k in range(1, NY):
        to = lax.rem(y + k, 8)
        copy = remote(yb.at[to], ybrecv.at[k - 1], s_yb.at[k - 1], r_yb.at[k - 1], at_y(k))
        ybs.append(copy)

        @pl.when((c == 0) | (to >= 4))
        def _():
            copy.start()

    ya[...] = gko[...].reshape(NY, 32, 576).astype(BF16)
    for k in range(1, NY):
        to = lax.rem(y + k, 8)
        copy = remote(ya.at[to], yarecv.at[k - 1], s_ya.at[k - 1], r_ya.at[k - 1], at_y(k))
        copy.start()
        yas.append(copy)

    def query_grad(par):
        return dot(gs[par], win[pl.ds(64 - 64 * par, 640), :], 1, 1)

    even = query_grad(0)
    stage_z(0)
    odd = query_grad(1)
    for i in range(4):
        rows = slice(i * 128, (i + 1) * 128)
        gqv[:, pl.ds(i * 1152, 512)] = even[rows, :512].astype(BF16)
        gqv[:, pl.ds(i * 1152 + 512, 128)] = (even[rows, 512:] + odd[rows, :128]).astype(BF16)
        gqv[:, pl.ds(i * 1152 + 640, 512)] = odd[rows, 128:].astype(BF16)
    store = pltpu.make_async_copy(gqv, gq_hbm, s_out)
    store.start()
    stage_z(1)

    back = remote(
        bsend, brecv, s_b, r_b, ring(jnp.where((c == 1) | (y >= 4), -2, -1))
    )

    @pl.when((c == 0) | (y >= 4))
    def _():
        mine = yb[y].astype(F32)
        for k in range(1, NY):
            ybs[k - 1].wait_recv()
            mine = mine + ybrecv[k - 1].astype(F32)
        bsend[...] = mine.astype(BF16)
        back.start()

    stage_swap(0)
    mine = ya[y].astype(F32)
    for k in range(1, NY):
        yas[k - 1].wait_recv()
        mine = mine + yarecv[k - 1].astype(F32)
    gl_ref[...] = mine

    @pl.when((c == 1) | (y >= 4))
    def _():
        back.wait_recv()
        gl_ref[...] += brecv[...].astype(F32)

    stage_swap(1)
    for par in range(2):
        for side in range(2):
            half_of = c if side == 0 else 1 - c
            if side == 1:
                swaps[par].wait_recv()
            value = fin[par, c] if side == 0 else frecv[par]
            for i in range(2):
                col = half_of * 512 + i * 256 + par * 128
                gw_ref[:, pl.ds(pl.multiple_of(col, 128), 128)] = value[:, i * 128 : i * 128 + 128]

    near.wait_send()
    far.wait_send()

    @pl.when(c == 1)
    def _():
        whole.wait_send()

    @pl.when(c == 0)
    def _():
        half.wait_send()

    for k in range(1, NY):
        @pl.when((c == 0) | (lax.rem(y + k, 8) >= 4))
        def _():
            ybs[k - 1].wait_send()

    @pl.when((c == 0) | (y >= 4))
    def _():
        back.wait_send()

    for copy in yas + cores[0] + cores[1] + xs[0] + xs[1] + zs[0] + zs[1] + swaps:
        copy.wait_send()
    store.wait()


def on_device(queries, latents, up_value, grad_out, out_saved, log_sums, doc_starts):
    anywhere = pl.BlockSpec(memory_space=pl.ANY)
    vmem = pl.BlockSpec(memory_space=pltpu.VMEM)
    dma = pltpu.SemaphoreType.DMA
    shapes = [
        ((128, 4608), BF16), ((512, 1024), BF16), ((128, 1024), BF16), ((128, 1024), BF16),
        ((8, 128), F32), ((704, 640), BF16), ((2, 512, 640), BF16), ((2, 512, 512), BF16),
        ((2, 512, 640), BF16), ((2, 512, 640), BF16), ((2, 512, 512), F32), ((128, 4608), BF16),
        ((128, 8), F32), ((128, 8), F32),
        ((256, 576), F32), ((256, 576), BF16), ((256, 576), BF16),
        ((NY, 32, 576), BF16), ((NY - 1, 32, 576), BF16),
        ((NY, 32, 576), BF16), ((NY - 1, 32, 576), BF16),
        ((32, 576), F32), ((32, 576), BF16), ((32, 576), BF16),
        ((2, 2, NX, NZ, 16, 256), BF16), ((2, NX, NZ, 16, 256), BF16),
        ((2 * (NX - 1), NZ, 16, 256), BF16), ((2 * (NX - 1), NZ, 16, 256), BF16),
        ((2, NZ, 16, 256), F32), ((2, NZ, 16, 256), BF16), ((2 * (NZ - 1), 16, 256), BF16),
        ((2, 2, 8, 256), F32), ((2, 8, 256), F32),
    ]
    return pl.pallas_call(
        kernel,
        out_shape=(
            jax.ShapeDtypeStruct((128, 4608), BF16),
            jax.ShapeDtypeStruct((32, 576), F32),
            jax.ShapeDtypeStruct((8, 1024), F32),
        ),
        in_specs=[anywhere] * 6 + [vmem],
        out_specs=(anywhere, vmem, vmem),
        scratch_shapes=[pltpu.VMEM(shape, kind) for shape, kind in shapes]
        + [
            dma((6,)), dma, dma((2,)), dma((2,)), dma, dma,
            dma((NY - 1,)), dma((NY - 1,)), dma((NY - 1,)), dma((NY - 1,)), dma, dma,
            dma((2 * NX,)), dma((2 * NX,)), dma((2 * NX - 2,)), dma((2 * NX - 2,)),
            dma((2 * NZ - 2,)), dma((2 * NZ - 2,)), dma((2,)), dma((2,)),
        ],
        compiler_params=pltpu.CompilerParams(
            collective_id=0, has_side_effects=True, vmem_limit_bytes=58 << 20
        ),
        name="latent_attention_backward",
    )(queries, latents.T, up_value, grad_out, out_saved, log_sums.T, doc_starts.reshape(1, -1))


def solution(mesh):
    return jax.shard_map(
        on_device,
        mesh=mesh,
        in_specs=(
            P("ctx", "head"),
            P("ctx", None),
            P(None, "head"),
            P("ctx", "head"),
            P("ctx", "head"),
            P("ctx", "head"),
            P(),
        ),
        out_specs=(P("ctx", "head"), P(("ctx", "head"), None), P("ctx", "head")),
        check_vma=False,
    )
```

time: 264 us -> 53.2 us (0.20)
  waiting for transfers between devices: 188 us -> 0 us
  Pallas kernels: 0 us -> 47.4 us
  matrix products: 30.9 us -> 0 us
  between operations: 16.6 us -> 0.66 us
  starting transfers between devices: 14.4 us -> 0 us
  local copies, waits for them, and re-layouts: 9.47 us -> 4.9 us
  other arithmetic: 3.26 us -> 0 us
    unnamed x3 -> x0, waiting for transfers between devices: 179 us -> none
    pallas_call x0 -> x1, Pallas kernels: none -> 47.4 us  [on_device(): pl.pallas_call(kernel, out_shape=(jax.ShapeDtypeStruct((128, 4608), BF16)...]
    dot_general x19 -> x0, matrix products: 30.9 us -> none  [the longest x3 5.99 us: one_task(): jnp.einsum('thf,sf->ths', query_heads, key_block, preferred_element_type=...]
    ppermute x4 -> x0, starting transfers between devices: 14.3 us -> none  [passed_along(): lax.ppermute(value, axis, [(source, source + steps) for source in range(f...]
    ppermute x4 -> x0, waiting for transfers between devices: 9.23 us -> none  [passed_along(): lax.ppermute(value, axis, [(source, source + steps) for source in range(f...]
    unnamed x50 -> x7, local copies, waits for them, and re-layouts: 6.29 us -> 3.65 us
  transfers between devices with their start and end apart: 6 -> 0, of which waited for: 2 -> 0; matrix products, arithmetic and copies ran while one was open for 16% -> 0% of each run, Pallas kernels for 0% -> 0%
where the time goes in v2:
time: 53.2 us; the launch traced here: 53 us
  Pallas kernels  47.4 us (89%)
  local copies, waits for them, and re-layouts  4.9 us (9%)
  between operations  0.66 us (1%)
    pallas_call x1, Pallas kernels, on_device(): pl.pallas_call(kernel, out_shape=(jax.ShapeDtypeStruct((128, 4608), BF16)...  47.4 us
    unnamed x7, local copies, waits for them, and re-layouts  3.65 us
    reshape x1, local copies, waits for them, and re-layouts, on_device(): doc_starts.reshape(1, -1)  1.25 us

profile of v2, /device:TPU:1, one launch (start us, length us, event | category | flops | bytes accessed | tf_op | source)
XLA Modules:
  0.0 53.0 jit_solution(12477162294559483838)
XLA Ops:
  0.6 1.2 %reshape.9.ds_ref = s32[1,257]{1,0:T(1,128)} reshape(s32[257]{0:T(512)} %param.13) | data formatting | bytes 2056 | tf_op jit(solution)/shard_map/reshape | solution.py:349
  1.9 47.4 %latent_attention_backward.1 = (bf16[128,4608]{1,0:T(8,128)(2,1)}, f32[32,576]{1,0:T(8,128)}, f32[8,1024]{1,0:T(8,128)}) custom-call(bf16[128,4608]{1,0:T(8,128)(2,1)} %q_hbm.1, bf16[576,256]{1,0:T(8,128)(2,1)} %bitcast.2, bf16[512,1024]{1,0:T(8,128)(2,1)} %w_hbm.1, bf16[128,1024]{1,0:T(8,128)(2,1)} %g_hbm.1, bf16[128,1024]{1,0:T(8,128)(2,1)} %o_hbm.1, ...), custom_call_target="tpu_custom_call" | custom-call | tf_op jit(solution)/shard_map/latent_attention_backward/pallas_call | solution.py:329
  49.3 0.0 copy-start
  49.3 0.0 copy-start.1
  49.3 2.4 %copy.13 = bf16[128,4608]{1,0:T(8,128)(2,1)} copy(bf16[128,4608]{1,0:T(8,128)(2,1)} %get-tuple-element.6) | data formatting | bytes 2359296
  51.7 0.0 copy-done
  51.7 0.6 %copy.14 = f32[32,576]{1,0:T(8,128)} copy(f32[32,576]{1,0:T(8,128)S(1)} %copy-done) | data formatting | bytes 147456
  52.4 0.0 copy-done.1
  52.4 0.6 %copy.15 = f32[8,1024]{1,0:T(8,128)} copy(f32[8,1024]{1,0:T(8,128)S(1)} %copy-done.1) | data formatting | bytes 65536
Async XLA Ops:
  49.3 2.4 %copy-start = (f32[32,576]{1,0:T(8,128)S(1)}, f32[32,576]{1,0:T(8,128)}, u32[]{:S(2)}) copy-start(f32[32,576]{1,0:T(8,128)} %get-tuple-element.7) | copy-start | bytes 221188
  49.3 3.0 %copy-start.1 = (f32[8,1024]{1,0:T(8,128)S(1)}, f32[8,1024]{1,0:T(8,128)}, u32[]{:S(2)}) copy-start(f32[8,1024]{1,0:T(8,128)} %get-tuple-element.8) | copy-start | bytes 98308

commit v3 on v2

--- a/solution.py
+++ b/solution.py
@@ -87,7 +87,7 @@
                 gv[:, cols].astype(F32) * ov[:, cols].astype(F32), axis=1, keepdims=True
             )
     qpos = d * 256 + 128 + lax.broadcasted_iota(jnp.int32, (128, 1), 0)
-    starts = ds_ref[...]
+    starts = ds_ref[...].reshape(1, 257)
     begin = jnp.max(jnp.where(starts <= qpos, starts, 0), axis=1, keepdims=True)
 
     def attend(par, block, base):
@@ -119,9 +119,39 @@
         ol[par] = attend(par, OWN, d * 256)
     gko[...] = key_grad(OWN)
 
-    near.wait_recv()
-    for par in range(2):
-        ol[par] += attend(par, NEAR, d * 256 - 256)
+    whole = remote(nbuf, nrecv, s_n, r_n, partner)
+    half = remote(
+        nbuf.at[pl.ds(128, 128)], nrecv.at[pl.ds(0, 128)], s_n, r_n, partner
+    )
+
+    def attend_near():
+        near.wait_recv()
+        for par in range(2):
+            ol[par] += attend(par, NEAR, d * 256 - 256)
+
+    @pl.when(c == 1)
+    def _():
+        attend_near()
+        nbuf[...] = key_grad(NEAR).astype(BF16)
+        whole.start()
+
+    @pl.when(c == 0)
+    def _():
+        whole.wait_recv()
+        gko[...] += nrecv[...].astype(F32)
+
+    ya[...] = gko[...].reshape(NY, 32, 576).astype(BF16)
+    ybs, yas = [], []
+    for k in range(1, NY):
+        to = lax.rem(y + k, 8)
+        copy = remote(ya.at[to], yarecv.at[k - 1], s_ya.at[k - 1], r_ya.at[k - 1], at_y(k))
+        copy.start()
+        yas.append(copy)
+
+    @pl.when(c == 0)
+    def _():
+        attend_near()
+
     far.wait_recv()
 
     cores, xs, zs, swaps = [[], []], [[], []], [[], []], []
@@ -183,29 +213,18 @@
     up_grad(1)
     stage_x(0)
 
-    near_grad = key_grad(NEAR)
-    nbuf[...] = near_grad.astype(BF16)
-    whole = remote(nbuf, nrecv, s_n, r_n, partner)
-    half = remote(
-        nbuf.at[pl.ds(128, 128)], nrecv.at[pl.ds(0, 128)], s_n, r_n, partner
-    )
-
-    @pl.when(c == 1)
-    def _():
-        whole.start()
-
     @pl.when(c == 0)
     def _():
+        near_grad = key_grad(NEAR)
+        nbuf[...] = near_grad.astype(BF16)
         half.start()
+        yb[pl.ds(0, 4)] = near_grad[:128].reshape(4, 32, 576).astype(BF16)
 
     stage_x(1)
     gkf = key_grad(FAR)
-    yb[pl.ds(0, 4)] = near_grad[:128].reshape(4, 32, 576).astype(BF16)
 
     @pl.when(c == 0)
     def _():
-        whole.wait_recv()
-        gko[...] += nrecv[...].astype(F32)
         yb[pl.ds(4, 4)] = gkf.reshape(4, 32, 576).astype(BF16)
 
     @pl.when(c == 1)
@@ -215,7 +234,6 @@
             (gkf + nrecv[pl.ds(0, 128)].astype(F32)).reshape(4, 32, 576).astype(BF16)
         )
 
-    ybs, yas = [], []
     for k in range(1, NY):
         to = lax.rem(y + k, 8)
         copy = remote(yb.at[to], ybrecv.at[k - 1], s_yb.at[k - 1], r_yb.at[k - 1], at_y(k))
@@ -224,13 +242,6 @@
         @pl.when((c == 0) | (to >= 4))
         def _():
             copy.start()
-
-    ya[...] = gko[...].reshape(NY, 32, 576).astype(BF16)
-    for k in range(1, NY):
-        to = lax.rem(y + k, 8)
-        copy = remote(ya.at[to], yarecv.at[k - 1], s_ya.at[k - 1], r_ya.at[k - 1], at_y(k))
-        copy.start()
-        yas.append(copy)
 
     def query_grad(par):
         return dot(gs[par], win[pl.ds(64 - 64 * par, 640), :], 1, 1)
@@ -306,6 +317,22 @@
     for copy in yas + cores[0] + cores[1] + xs[0] + xs[1] + zs[0] + zs[1] + swaps:
         copy.wait_send()
     store.wait()
+
+
+def settle_kernel(gq_in, gl_in, gw_in, gq_out, gl_out, gw_out, gqv, glv, gwv, s_in, s_out):
+    parts = [(gl_in, glv, gl_out), (gw_in, gwv, gw_out)]
+    for i in range(8):
+        rows = pl.ds(16 * i, 16)
+        parts.append((gq_in.at[rows], gqv.at[rows], gq_out.at[rows]))
+    reads = [pltpu.make_async_copy(a, v, s_in.at[i]) for i, (a, v, _) in enumerate(parts)]
+    writes = [pltpu.make_async_copy(v, b, s_out.at[i]) for i, (_, v, b) in enumerate(parts)]
+    for read in reads:
+        read.start()
+    for read, write in zip(reads, writes):
+        read.wait()
+        write.start()
+    for write in writes:
+        write.wait()
 
 
 def on_device(queries, latents, up_value, grad_out, out_saved, log_sums, doc_starts):
@@ -326,7 +353,7 @@
         ((2, NZ, 16, 256), F32), ((2, NZ, 16, 256), BF16), ((2 * (NZ - 1), 16, 256), BF16),
         ((2, 2, 8, 256), F32), ((2, 8, 256), F32),
     ]
-    return pl.pallas_call(
+    results = pl.pallas_call(
         kernel,
         out_shape=(
             jax.ShapeDtypeStruct((128, 4608), BF16),
@@ -346,7 +373,15 @@
             collective_id=0, has_side_effects=True, vmem_limit_bytes=58 << 20
         ),
         name="latent_attention_backward",
-    )(queries, latents.T, up_value, grad_out, out_saved, log_sums.T, doc_starts.reshape(1, -1))
+    )(queries, latents.T, up_value, grad_out, out_saved, log_sums.T, doc_starts)
+    return pl.pallas_call(
+        settle_kernel,
+        out_shape=tuple(jax.ShapeDtypeStruct(r.shape, r.dtype) for r in results),
+        in_specs=[anywhere] * 3,
+        out_specs=(anywhere,) * 3,
+        scratch_shapes=[pltpu.VMEM(r.shape, r.dtype) for r in results] + [dma((10,)), dma((10,))],
+        name="settle",
+    )(*results)
 
 
 def solution(mesh):

time: 53.2 us -> 47.1 us (0.89)
  local copies, waits for them, and re-layouts: 4.9 us -> 0 us
  Pallas kernels: 47.4 us -> 46.3 us
    unnamed x7 -> x0, local copies, waits for them, and re-layouts: 3.65 us -> none
    pallas_call x1, Pallas kernels: 47.4 us -> 44.1 us  [on_device(): pl.pallas_call(kernel, out_shape=(jax.ShapeDtypeStruct((128, 4608), BF16)...]
    pallas_call x0 -> x1, Pallas kernels: none -> 2.22 us  [on_device(): pl.pallas_call(settle_kernel, out_shape=tuple((jax.ShapeDtypeStruct(r.sha...]
    reshape x1 -> x0, local copies, waits for them, and re-layouts: 1.25 us -> none  [on_device(): doc_starts.reshape(1, -1)]
where the time goes in v3:
time: 47.1 us; the launch traced here: 46.9 us
  Pallas kernels  46.3 us (98%)
  between operations  0.64 us (1%)
    pallas_call x1, Pallas kernels, on_device(): pl.pallas_call(kernel, out_shape=(jax.ShapeDtypeStruct((128, 4608), BF16)...  44.1 us
    pallas_call x1, Pallas kernels, on_device(): pl.pallas_call(settle_kernel, out_shape=tuple((jax.ShapeDtypeStruct(r.sha...  2.22 us

profile of v3, /device:TPU:1, one launch (start us, length us, event | category | flops | bytes accessed | tf_op | source)
XLA Modules:
  0.0 46.9 jit_solution(4527811777056912532)
XLA Ops:
  0.6 44.1 %latent_attention_backward.1 = (bf16[128,4608]{1,0:T(8,128)(2,1)}, f32[32,576]{1,0:T(8,128)}, f32[8,1024]{1,0:T(8,128)}) custom-call(bf16[128,4608]{1,0:T(8,128)(2,1)} %q_hbm.1, bf16[576,256]{1,0:T(8,128)(2,1)} %bitcast.2, bf16[512,1024]{1,0:T(8,128)(2,1)} %w_hbm.1, bf16[128,1024]{1,0:T(8,128)(2,1)} %g_hbm.1, bf16[128,1024]{1,0:T(8,128)(2,1)} %o_hbm.1, ...), custom_call_target="tpu_custom_call" | custom-call | tf_op jit(solution)/shard_map/latent_attention_backward/pallas_call | solution.py:356
  44.7 2.2 %settle.1 = (bf16[128,4608]{1,0:T(8,128)(2,1)}, f32[32,576]{1,0:T(8,128)}, f32[8,1024]{1,0:T(8,128)}) custom-call(bf16[128,4608]{1,0:T(8,128)(2,1)} %get-tuple-element.6.gq_in, f32[32,576]{1,0:T(8,128)} %get-tuple-element.7.gl_in, f32[8,1024]{1,0:T(8,128)} %get-tuple-element.8.gw_in), custom_call_target="tpu_custom_call" | custom-call | tf_op jit(solution)/shard_map/settle/pallas_call | solution.py:377

commit v4 on v3

--- a/solution.py
+++ b/solution.py
@@ -24,7 +24,7 @@
     gko, nbuf, nrecv, ya, yarecv, yb, ybrecv, ybsum, bsend, brecv,
     tv, crecv, xsend, xrecv, zpart, zsend, zrecv, fin, frecv,
     s_in, s_out, s_sh, r_sh, s_n, r_n, s_ya, r_ya, s_yb, r_yb, s_b, r_b,
-    s_c, r_c, s_x, r_x, s_z, r_z, s_f, r_f,
+    s_c, r_c, s_x, r_x, s_z, r_z, s_f, r_f, known,
 ):
     d, y = lax.axis_index("ctx"), lax.axis_index("head")
     z, x, c = d // 8, lax.rem(d // 2, 4), lax.rem(d, 2)
@@ -49,11 +49,19 @@
     for load in loads:
         load.start()
 
+    sides = [at_y(1), at_y(NY - 1), at_z(1), at_z(NZ - 1)]
+
+    def tell(level):
+        for side in sides:
+            pl.semaphore_signal(known.at[level], inc=1, device_id=side, device_id_type=MESH)
+
+    def hear(level):
+        pl.semaphore_wait(known.at[level], len(sides))
+
     peers = (
         [ring(1), ring(-1), ring(2), ring(-2), partner]
         + [at_x(k) for k in range(1, NX)]
-        + [at_y(k) for k in range(1, NY)]
-        + [at_z(k) for k in range(1, NZ)]
+        + sides
     )
     entry = pltpu.get_barrier_semaphore()
     for peer in peers:
@@ -72,6 +80,7 @@
     )
     near.start()
     far.start()
+    tell(0)
 
     for load in loads[1:]:
         load.wait()
@@ -115,42 +124,51 @@
         both = even + odd
         return jnp.concatenate([both[:, :512] + value, both[:, 512:576]], axis=1)
 
-    for par in range(2):
-        ol[par] = attend(par, OWN, d * 256)
+    ol[0] = attend(0, OWN, d * 256)
+    hear(0)
+    tell(1)
+    ol[1] = attend(1, OWN, d * 256)
+    hear(1)
+    tell(2)
     gko[...] = key_grad(OWN)
+    hear(2)
 
     whole = remote(nbuf, nrecv, s_n, r_n, partner)
-    half = remote(
-        nbuf.at[pl.ds(128, 128)], nrecv.at[pl.ds(0, 128)], s_n, r_n, partner
-    )
-
-    def attend_near():
+    half = remote(nbuf.at[pl.ds(128, 128)], nrecv.at[pl.ds(0, 128)], s_n, r_n, partner)
+    yas = [
+        remote(
+            ya.at[lax.rem(y + k, 8)], yarecv.at[k - 1], s_ya.at[k - 1], r_ya.at[k - 1], at_y(k)
+        )
+        for k in range(1, NY)
+    ]
+    ybs = [
+        remote(
+            yb.at[lax.rem(y + k, 8)], ybrecv.at[k - 1], s_yb.at[k - 1], r_yb.at[k - 1], at_y(k)
+        )
+        for k in range(1, NY)
+    ]
+
+    def send_own():
+        ya[...] = gko[...].reshape(NY, 32, 576).astype(BF16)
+        for copy in yas:
+            copy.start()
+
+    def attend_near(par):
+        ol[par] += attend(par, NEAR, d * 256 - 256)
+
+    @pl.when(c == 1)
+    def _():
+        send_own()
         near.wait_recv()
-        for par in range(2):
-            ol[par] += attend(par, NEAR, d * 256 - 256)
-
-    @pl.when(c == 1)
-    def _():
-        attend_near()
+        attend_near(0)
+        attend_near(1)
         nbuf[...] = key_grad(NEAR).astype(BF16)
         whole.start()
 
     @pl.when(c == 0)
     def _():
-        whole.wait_recv()
-        gko[...] += nrecv[...].astype(F32)
-
-    ya[...] = gko[...].reshape(NY, 32, 576).astype(BF16)
-    ybs, yas = [], []
-    for k in range(1, NY):
-        to = lax.rem(y + k, 8)
-        copy = remote(ya.at[to], yarecv.at[k - 1], s_ya.at[k - 1], r_ya.at[k - 1], at_y(k))
-        copy.start()
-        yas.append(copy)
-
-    @pl.when(c == 0)
-    def _():
-        attend_near()
+        near.wait_recv()
+        attend_near(0)
 
     far.wait_recv()
 
@@ -210,8 +228,16 @@
         swaps.append(copy)
 
     up_grad(0)
+
+    @pl.when(c == 0)
+    def _():
+        attend_near(1)
+        whole.wait_recv()
+        gko[...] += nrecv[...].astype(F32)
+        send_own()
+
+    stage_x(0)
     up_grad(1)
-    stage_x(0)
 
     @pl.when(c == 0)
     def _():
@@ -219,9 +245,13 @@
         nbuf[...] = near_grad.astype(BF16)
         half.start()
         yb[pl.ds(0, 4)] = near_grad[:128].reshape(4, 32, 576).astype(BF16)
-
+        for k in range(1, NY):
+            @pl.when(lax.rem(y + k, 8) < 4)
+            def _():
+                ybs[k - 1].start()
+
+    gkf = key_grad(FAR)
     stage_x(1)
-    gkf = key_grad(FAR)
 
     @pl.when(c == 0)
     def _():
@@ -235,13 +265,9 @@
         )
 
     for k in range(1, NY):
-        to = lax.rem(y + k, 8)
-        copy = remote(yb.at[to], ybrecv.at[k - 1], s_yb.at[k - 1], r_yb.at[k - 1], at_y(k))
-        ybs.append(copy)
-
-        @pl.when((c == 0) | (to >= 4))
+        @pl.when(lax.rem(y + k, 8) >= 4)
         def _():
-            copy.start()
+            ybs[k - 1].start()
 
     def query_grad(par):
         return dot(gs[par], win[pl.ds(64 - 64 * par, 640), :], 1, 1)
@@ -251,11 +277,9 @@
     odd = query_grad(1)
     for i in range(4):
         rows = slice(i * 128, (i + 1) * 128)
-        gqv[:, pl.ds(i * 1152, 512)] = even[rows, :512].astype(BF16)
-        gqv[:, pl.ds(i * 1152 + 512, 128)] = (even[rows, 512:] + odd[rows, :128]).astype(BF16)
-        gqv[:, pl.ds(i * 1152 + 640, 512)] = odd[rows, 128:].astype(BF16)
-    store = pltpu.make_async_copy(gqv, gq_hbm, s_out)
-    store.start()
+        gq_hbm[:, pl.ds(i * 1152, 512)] = even[rows, :512].astype(BF16)
+        gq_hbm[:, pl.ds(i * 1152 + 512, 128)] = (even[rows, 512:] + odd[rows, :128]).astype(BF16)
+        gq_hbm[:, pl.ds(i * 1152 + 640, 512)] = odd[rows, 128:].astype(BF16)
     stage_z(1)
 
     back = remote(
@@ -316,20 +340,12 @@
 
     for copy in yas + cores[0] + cores[1] + xs[0] + xs[1] + zs[0] + zs[1] + swaps:
         copy.wait_send()
-    store.wait()
-
-
-def settle_kernel(gq_in, gl_in, gw_in, gq_out, gl_out, gw_out, gqv, glv, gwv, s_in, s_out):
-    parts = [(gl_in, glv, gl_out), (gw_in, gwv, gw_out)]
-    for i in range(8):
-        rows = pl.ds(16 * i, 16)
-        parts.append((gq_in.at[rows], gqv.at[rows], gq_out.at[rows]))
-    reads = [pltpu.make_async_copy(a, v, s_in.at[i]) for i, (a, v, _) in enumerate(parts)]
-    writes = [pltpu.make_async_copy(v, b, s_out.at[i]) for i, (_, v, b) in enumerate(parts)]
-    for read in reads:
-        read.start()
-    for read, write in zip(reads, writes):
-        read.wait()
+
+
+def settle_kernel(gq_in, gl_in, gw_in, gq_out, gl_out, gw_out, sem):
+    pairs = [(gq_in, gq_out), (gl_in, gl_out), (gw_in, gw_out)]
+    writes = [pltpu.make_async_copy(a, b, sem.at[i]) for i, (a, b) in enumerate(pairs)]
+    for write in writes:
         write.start()
     for write in writes:
         write.wait()
@@ -356,18 +372,19 @@
     results = pl.pallas_call(
         kernel,
         out_shape=(
-            jax.ShapeDtypeStruct((128, 4608), BF16),
-            jax.ShapeDtypeStruct((32, 576), F32),
-            jax.ShapeDtypeStruct((8, 1024), F32),
+            pltpu.VMEM((128, 4608), BF16),
+            pltpu.VMEM((32, 576), F32),
+            pltpu.VMEM((8, 1024), F32),
         ),
         in_specs=[anywhere] * 6 + [vmem],
-        out_specs=(anywhere, vmem, vmem),
+        out_specs=(vmem, vmem, vmem),
         scratch_shapes=[pltpu.VMEM(shape, kind) for shape, kind in shapes]
         + [
             dma((6,)), dma, dma((2,)), dma((2,)), dma, dma,
             dma((NY - 1,)), dma((NY - 1,)), dma((NY - 1,)), dma((NY - 1,)), dma, dma,
             dma((2 * NX,)), dma((2 * NX,)), dma((2 * NX - 2,)), dma((2 * NX - 2,)),
             dma((2 * NZ - 2,)), dma((2 * NZ - 2,)), dma((2,)), dma((2,)),
+            pltpu.SemaphoreType.REGULAR((3,)),
         ],
         compiler_params=pltpu.CompilerParams(
             collective_id=0, has_side_effects=True, vmem_limit_bytes=58 << 20
@@ -377,11 +394,11 @@
     return pl.pallas_call(
         settle_kernel,
         out_shape=tuple(jax.ShapeDtypeStruct(r.shape, r.dtype) for r in results),
-        in_specs=[anywhere] * 3,
+        in_specs=[vmem] * 3,
         out_specs=(anywhere,) * 3,
-        scratch_shapes=[pltpu.VMEM(r.shape, r.dtype) for r in results] + [dma((10,)), dma((10,))],
+        scratch_shapes=[dma((3,))],
         name="settle",
-    )(*results)
+    )(*[pltpu.with_memory_space_constraint(r, pltpu.VMEM) for r in results])
 
 
 def solution(mesh):

time: 47.1 us -> 42.6 us (0.904)
  the two profiles are of different devices: /device:TPU:1 before, /device:TPU:49 now
where the time goes in v4:
time: 42.6 us; the launch traced here: 42.5 us
  Pallas kernels  41.8 us (98%)
  between operations  0.64 us (2%)
    pallas_call x1, Pallas kernels, on_device(): pl.pallas_call(kernel, out_shape=(pltpu.VMEM((128, 4608), BF16), pltpu.VM...  40.8 us
    pallas_call x1, Pallas kernels, on_device(): pl.pallas_call(settle_kernel, out_shape=tuple((jax.ShapeDtypeStruct(r.sha...  1.06 us

profile of v4, /device:TPU:49, one launch (start us, length us, event | category | flops | bytes accessed | tf_op | source)
XLA Modules:
  0.0 42.5 jit_solution(8961616363422204556)
XLA Ops:
  0.6 40.8 %latent_attention_backward.1 = (bf16[128,4608]{1,0:T(8,128)(2,1)S(1)}, f32[32,576]{1,0:T(8,128)S(1)}, f32[8,1024]{1,0:T(8,128)S(1)}) custom-call(bf16[128,4608]{1,0:T(8,128)(2,1)} %q_hbm.1, bf16[576,256]{1,0:T(8,128)(2,1)} %bitcast.2, bf16[512,1024]{1,0:T(8,128)(2,1)} %w_hbm.1, bf16[128,1024]{1,0:T(8,128)(2,1)} %g_hbm.1, bf16[128,1024]{1,0:T(8,128)(2,1)} %o_hbm.1, ...), custom_call_target="tpu_custom_call" | custom-call | tf_op jit(solution)/shard_map/latent_attention_backward/pallas_call | solution.py:372
  41.4 1.1 %settle.1 = (bf16[128,4608]{1,0:T(8,128)(2,1)}, f32[32,576]{1,0:T(8,128)}, f32[8,1024]{1,0:T(8,128)}) custom-call(bf16[128,4608]{1,0:T(8,128)(2,1)S(1)} %get-tuple-element.6.gq_in, f32[32,576]{1,0:T(8,128)S(1)} %get-tuple-element.7.gl_in, f32[8,1024]{1,0:T(8,128)S(1)} %get-tuple-element.8.gw_in), custom_call_target="tpu_custom_call" | custom-call | tf_op jit(solution)/shard_map/settle/pallas_call | solution.py:394

commit v5 on v4

--- a/solution.py
+++ b/solution.py
@@ -22,9 +22,9 @@
     gq_hbm, gl_ref, gw_ref,
     qv, wv, gv, ov, lsv, win, qs, gl, pb, gs, ol, gqv, delta, lsc,
     gko, nbuf, nrecv, ya, yarecv, yb, ybrecv, ybsum, bsend, brecv,
-    tv, crecv, xsend, xrecv, zpart, zsend, zrecv, fin, frecv,
+    tv, crecv, xsend, xrecv, zpart, zsend, zrecv,
     s_in, s_out, s_sh, r_sh, s_n, r_n, s_ya, r_ya, s_yb, r_yb, s_b, r_b,
-    s_c, r_c, s_x, r_x, s_z, r_z, s_f, r_f, known,
+    s_c, r_c, s_x, r_x, s_z, r_z, known,
 ):
     d, y = lax.axis_index("ctx"), lax.axis_index("head")
     z, x, c = d // 8, lax.rem(d // 2, 4), lax.rem(d, 2)
@@ -172,16 +172,22 @@
 
     far.wait_recv()
 
-    cores, xs, zs, swaps = [[], []], [[], []], [[], []], []
+    cores, xs, zs = [[], []], [[], []], [[], []]
 
     def up_grad(par):
         lat = (ol[par] + attend(par, FAR, d * 256 - 384)).astype(BF16)
-        for i in range(4):
-            h = 2 * i + par
-            term = dot(lat[i * 128 : (i + 1) * 128], gv[:, pl.ds(h * 128, 128)], 0, 0)
-            term = term.astype(BF16).reshape(NZ, NX, 16, 128)
+        for i in range(2):
+            low, high = [
+                dot(
+                    lat[j * 128 : (j + 1) * 128], gv[:, pl.ds((2 * j + par) * 128, 128)], 0, 0
+                ).reshape(NZ * NX * NC, 8, 128)
+                for j in (i, i + 2)
+            ]
+            term = jnp.concatenate([low, high], axis=1).astype(BF16)
+            term = term.reshape(NZ, NX, NC, 16, 128)
             for xi in range(NX):
-                tv[par, i // 2, xi, :, :, pl.ds((i % 2) * 128, 128)] = term[:, xi]
+                for ci in range(NC):
+                    tv[par, ci, xi, :, :, pl.ds(i * 128, 128)] = term[:, xi, ci]
         for k in range(1, NX + 1):
             xi = lax.rem(x + k, 4)
             j = par * NX + k - 1
@@ -217,15 +223,16 @@
             copy.start()
             zs[par].append(copy)
 
-    def stage_swap(par):
+    def finish(par):
         last = zsend[par, z].astype(F32)
         for k in range(1, NZ):
             zs[par][k - 1].wait_recv()
             last = last + zrecv[par * (NZ - 1) + k - 1].astype(F32)
-        fin[par] = last.reshape(2, 8, 256)
-        copy = remote(fin.at[par, 1 - c], frecv.at[par], s_f.at[par], r_f.at[par], partner)
-        copy.start()
-        swaps.append(copy)
+        for side in range(2):
+            for i in range(2):
+                gw_ref[:, pl.ds((2 * i + par + 4 * side) * 128, 128)] = last[
+                    side * 8 : side * 8 + 8, i * 128 : i * 128 + 128
+                ]
 
     up_grad(0)
 
@@ -295,7 +302,7 @@
         bsend[...] = mine.astype(BF16)
         back.start()
 
-    stage_swap(0)
+    finish(0)
     mine = ya[y].astype(F32)
     for k in range(1, NY):
         yas[k - 1].wait_recv()
@@ -307,17 +314,7 @@
         back.wait_recv()
         gl_ref[...] += brecv[...].astype(F32)
 
-    stage_swap(1)
-    for par in range(2):
-        for side in range(2):
-            half_of = c if side == 0 else 1 - c
-            if side == 1:
-                swaps[par].wait_recv()
-            value = fin[par, c] if side == 0 else frecv[par]
-            for i in range(2):
-                col = half_of * 512 + i * 256 + par * 128
-                gw_ref[:, pl.ds(pl.multiple_of(col, 128), 128)] = value[:, i * 128 : i * 128 + 128]
-
+    finish(1)
     near.wait_send()
     far.wait_send()
 
@@ -338,7 +335,7 @@
     def _():
         back.wait_send()
 
-    for copy in yas + cores[0] + cores[1] + xs[0] + xs[1] + zs[0] + zs[1] + swaps:
+    for copy in yas + cores[0] + cores[1] + xs[0] + xs[1] + zs[0] + zs[1]:
         copy.wait_send()
 
 
@@ -367,7 +364,6 @@
         ((2, 2, NX, NZ, 16, 256), BF16), ((2, NX, NZ, 16, 256), BF16),
         ((2 * (NX - 1), NZ, 16, 256), BF16), ((2 * (NX - 1), NZ, 16, 256), BF16),
         ((2, NZ, 16, 256), F32), ((2, NZ, 16, 256), BF16), ((2 * (NZ - 1), 16, 256), BF16),
-        ((2, 2, 8, 256), F32), ((2, 8, 256), F32),
     ]
     results = pl.pallas_call(
         kernel,
@@ -383,7 +379,7 @@
             dma((6,)), dma, dma((2,)), dma((2,)), dma, dma,
             dma((NY - 1,)), dma((NY - 1,)), dma((NY - 1,)), dma((NY - 1,)), dma, dma,
             dma((2 * NX,)), dma((2 * NX,)), dma((2 * NX - 2,)), dma((2 * NX - 2,)),
-            dma((2 * NZ - 2,)), dma((2 * NZ - 2,)), dma((2,)), dma((2,)),
+            dma((2 * NZ - 2,)), dma((2 * NZ - 2,)),
             pltpu.SemaphoreType.REGULAR((3,)),
         ],
         compiler_params=pltpu.CompilerParams(

time: 42.6 us -> 41.2 us (0.967)
  the two profiles are of different devices: /device:TPU:49 before, /device:TPU:48 now
where the time goes in v5:
time: 41.2 us; the launch traced here: 41.1 us
  Pallas kernels  40.4 us (98%)
  between operations  0.64 us (2%)
    pallas_call x1, Pallas kernels, on_device(): pl.pallas_call(kernel, out_shape=(pltpu.VMEM((128, 4608), BF16), pltpu.VM...  39.4 us
    pallas_call x1, Pallas kernels, on_device(): pl.pallas_call(settle_kernel, out_shape=tuple((jax.ShapeDtypeStruct(r.sha...  1.06 us

profile of v5, /device:TPU:48, one launch (start us, length us, event | category | flops | bytes accessed | tf_op | source)
XLA Modules:
  0.0 41.1 jit_solution(5673292130009150832)
XLA Ops:
  0.6 39.4 %latent_attention_backward.1 = (bf16[128,4608]{1,0:T(8,128)(2,1)S(1)}, f32[32,576]{1,0:T(8,128)S(1)}, f32[8,1024]{1,0:T(8,128)S(1)}) custom-call(bf16[128,4608]{1,0:T(8,128)(2,1)} %q_hbm.1, bf16[576,256]{1,0:T(8,128)(2,1)} %bitcast.2, bf16[512,1024]{1,0:T(8,128)(2,1)} %w_hbm.1, bf16[128,1024]{1,0:T(8,128)(2,1)} %g_hbm.1, bf16[128,1024]{1,0:T(8,128)(2,1)} %o_hbm.1, ...), custom_call_target="tpu_custom_call" | custom-call | tf_op jit(solution)/shard_map/latent_attention_backward/pallas_call | solution.py:368
  40.0 1.1 %settle.1 = (bf16[128,4608]{1,0:T(8,128)(2,1)}, f32[32,576]{1,0:T(8,128)}, f32[8,1024]{1,0:T(8,128)}) custom-call(bf16[128,4608]{1,0:T(8,128)(2,1)S(1)} %get-tuple-element.6.gq_in, f32[32,576]{1,0:T(8,128)S(1)} %get-tuple-element.7.gl_in, f32[8,1024]{1,0:T(8,128)S(1)} %get-tuple-element.8.gw_in), custom_call_target="tpu_custom_call" | custom-call | tf_op jit(solution)/shard_map/settle/pallas_call | solution.py:390

commit v6 on v5

--- a/solution.py
+++ b/solution.py
@@ -82,7 +82,14 @@
     far.start()
     tell(0)
 
-    for load in loads[1:]:
+    for load in loads[1:3]:
+        load.wait()
+    for par in range(2):
+        for i in range(4):
+            rows = pl.ds(i * 128, 128)
+            cols = pl.ds((2 * i + par) * 128, 128)
+            gl[par, rows, :] = dot(gv[:, cols], wv[:, cols], 1, 1).astype(BF16)
+    for load in loads[3:]:
         load.wait()
     lsc[...] = lsv[...].T
     for par in range(2):
@@ -91,7 +98,6 @@
             h = 2 * i + par
             cols = pl.ds(h * 128, 128)
             qs[par, rows, :] = qv[:, pl.ds(i * 1152 + par * 512, 640)]
-            gl[par, rows, :] = dot(gv[:, cols], wv[:, cols], 1, 1).astype(BF16)
             delta[:, pl.ds(h, 1)] = jnp.sum(
                 gv[:, cols].astype(F32) * ov[:, cols].astype(F32), axis=1, keepdims=True
             )
@@ -257,12 +263,20 @@
             def _():
                 ybs[k - 1].start()
 
+    def send_far():
+        for k in range(1, NY):
+            @pl.when(lax.rem(y + k, 8) >= 4)
+            def _():
+                ybs[k - 1].start()
+
     gkf = key_grad(FAR)
+
+    @pl.when(c == 0)
+    def _():
+        yb[pl.ds(4, 4)] = gkf.reshape(4, 32, 576).astype(BF16)
+        send_far()
+
     stage_x(1)
-
-    @pl.when(c == 0)
-    def _():
-        yb[pl.ds(4, 4)] = gkf.reshape(4, 32, 576).astype(BF16)
 
     @pl.when(c == 1)
     def _():
@@ -270,11 +284,7 @@
         yb[pl.ds(4, 4)] = (
             (gkf + nrecv[pl.ds(0, 128)].astype(F32)).reshape(4, 32, 576).astype(BF16)
         )
-
-    for k in range(1, NY):
-        @pl.when(lax.rem(y + k, 8) >= 4)
-        def _():
-            ybs[k - 1].start()
+        send_far()
 
     def query_grad(par):
         return dot(gs[par], win[pl.ds(64 - 64 * par, 640), :], 1, 1)

time: 41.2 us -> 41.3 us (level)
  no operation moved by 1% of the time
where the time goes in v6:
time: 41.3 us; the launch traced here: 41.1 us
  Pallas kernels  40.5 us (98%)
  between operations  0.64 us (2%)
    pallas_call x1, Pallas kernels, on_device(): pl.pallas_call(kernel, out_shape=(pltpu.VMEM((128, 4608), BF16), pltpu.VM...  39.4 us
    pallas_call x1, Pallas kernels, on_device(): pl.pallas_call(settle_kernel, out_shape=tuple((jax.ShapeDtypeStruct(r.sha...  1.06 us

profile of v6, /device:TPU:48, one launch (start us, length us, event | category | flops | bytes accessed | tf_op | source)
XLA Modules:
  0.0 41.1 jit_solution(13004508663387427300)
XLA Ops:
  0.6 39.4 %latent_attention_backward.1 = (bf16[128,4608]{1,0:T(8,128)(2,1)S(1)}, f32[32,576]{1,0:T(8,128)S(1)}, f32[8,1024]{1,0:T(8,128)S(1)}) custom-call(bf16[128,4608]{1,0:T(8,128)(2,1)} %q_hbm.1, bf16[576,256]{1,0:T(8,128)(2,1)} %bitcast.2, bf16[512,1024]{1,0:T(8,128)(2,1)} %w_hbm.1, bf16[128,1024]{1,0:T(8,128)(2,1)} %g_hbm.1, bf16[128,1024]{1,0:T(8,128)(2,1)} %o_hbm.1, ...), custom_call_target="tpu_custom_call" | custom-call | tf_op jit(solution)/shard_map/latent_attention_backward/pallas_call | solution.py:378
  40.0 1.1 %settle.1 = (bf16[128,4608]{1,0:T(8,128)(2,1)}, f32[32,576]{1,0:T(8,128)}, f32[8,1024]{1,0:T(8,128)}) custom-call(bf16[128,4608]{1,0:T(8,128)(2,1)S(1)} %get-tuple-element.6.gq_in, f32[32,576]{1,0:T(8,128)S(1)} %get-tuple-element.7.gl_in, f32[8,1024]{1,0:T(8,128)S(1)} %get-tuple-element.8.gw_in), custom_call_target="tpu_custom_call" | custom-call | tf_op jit(solution)/shard_map/settle/pallas_call | solution.py:400
